TPU v7x, 256 devices: a whole 4x4x8 slice. The times are simulated.
256 devices in a mesh: half: 2 (over core), cls: 2 (over y_lo), img: 64 (over y_hi, z, x).
Axes of the slice: x: 4, y: 4 (y_hi: 2, y_lo: 2; y = y_hi * 2 + y_lo), z: 8, core: 2. Of those that a mesh axis runs over, the one named last changes fastest.
Arguments:
- images: bfloat16 [2, 32768, 2, 8320], P('half', ('cls', 'img')), may hold values from -8 to 8
- projections: bfloat16 [2, 8, 8, 2, 8320], P('half', 'cls', None, None, 'img'), may hold values from -8 to 8
- ctf_table: float32 [2, 32, 8320], P('half'), may hold values from -1 to 1
- ctf_group: int32 [2, 32768], P('half', ('cls', 'img')), may hold values from 0 to 31
- orient_ids: int32 [2, 32768, 4], P('half', ('cls', 'img')), may hold values from 0 to 7
- trans_ids: int32 [2, 8], P('half'), may hold values from 0 to 24
- inv_sigma: float32 [2, 8320], P('half'), may hold values from 0.5 to 2
- counts: int32 [2, 128], P('half', ('cls', 'img')), may hold values from 1 to 256, 20480 in all within a row
Outputs:
- posterior: bfloat16 [2, 32768, 512], P('half', ('cls', 'img'))
- slab: float32 [2, 8, 8, 2, 8320], P('half', 'cls', None, None, 'img')
- fsc_map: float32 [2, 8, 8, 8320], P('half', 'cls', None, 'img')
Inputs may be any that keep to these rules, and one draw needn't show every extreme that they name: counts[h, s] is the number of live particles of shard s, held in its first slots; each half-set's counts sum to 20480, and the largest is 256.
All inputs are finite; a program needn't handle non-finite values.
Results may differ from a plain program's by a relative error of at most 0.013.
The roundings to bfloat16 on the way count: a program that leaves them out, or rounds other values in their place, can miss the bound.
Values may be sent and summed in bfloat16 or wider, within the bound.
No kernel may reach another device: no remote copies, remote signals or barrier semaphores. Data moves between devices by JAX's collectives and lax.ppermute only.
A program may use at most 192 MiB of HBM per device.

v0:
```python
import math
import jax
import jax.numpy as jnp
from jax import lax
from jax.sharding import PartitionSpec as P

K = 8
BOX = 128
O = 8
TR = 8
TGRID = 5


def swapped(value, axis, bit):
    return lax.ppermute(value, axis, [(i, i ^ 1 << bit) for i in range(lax.axis_size(axis))])


def phases(trans_list, count):
    half_width = BOX // 2 + 1
    freq_index = jnp.arange(count, dtype=jnp.int32)
    row_index = freq_index // half_width
    col_index = freq_index % half_width
    wave_x = (row_index - BOX * (row_index >= BOX // 2).astype(jnp.int32)).astype(jnp.float32)
    wave_y = col_index.astype(jnp.float32)
    shift_x = (trans_list % TGRID - TGRID // 2).astype(jnp.float32)
    shift_y = (trans_list // TGRID - TGRID // 2).astype(jnp.float32)
    angle = (
        2.0
        * math.pi
        / BOX
        * (shift_x[:, None] * wave_x[None, :] + shift_y[:, None] * wave_y[None, :])
    )
    return (jnp.cos(angle), jnp.sin(angle))


def shift_sections(sections, inverse, cosine, sine):
    real_part = sections[:, :, 0, :].astype(jnp.float32) * inverse
    imag_part = sections[:, :, 1, :].astype(jnp.float32) * inverse
    shifted_re = real_part[:, :, None, :] * cosine - imag_part[:, :, None, :] * sine
    shifted_im = real_part[:, :, None, :] * sine + imag_part[:, :, None, :] * cosine
    return jnp.stack([shifted_re, shifted_im], axis=3).astype(jnp.bfloat16)


def section_power(sections):
    real_part = sections[:, :, 0, :].astype(jnp.float32)
    imag_part = sections[:, :, 1, :].astype(jnp.float32)
    total = real_part * real_part + imag_part * imag_part
    return total.reshape(-1, total.shape[-1])


def contract_last(left, right):
    return lax.dot_general(
        left, right, (((1,), (1,)), ((), ())), preferred_element_type=jnp.float32
    )


def contract_high(left, right):
    return lax.dot_general(
        left,
        right,
        (((1,), (1,)), ((), ())),
        precision=lax.Precision.HIGHEST,
        preferred_element_type=jnp.float32,
    )


def on_device(images, projections, ctf_table, ctf_group, orient_ids, trans_ids, inv_sigma, counts):
    num_rows = images.shape[1]
    freqs = images.shape[3]
    groups = ctf_table.shape[1]
    inverse = inv_sigma[0]
    table = ctf_table[0]
    onehot = (ctf_group[0][:, None] == jnp.arange(groups, dtype=jnp.int32)[None, :]).astype(
        jnp.float32
    )
    ctf_rows = jnp.dot(
        onehot, table, precision=lax.Precision.HIGHEST, preferred_element_type=jnp.float32
    )
    weighted = (ctf_rows[:, None, :] * images[0].astype(jnp.float32)).astype(jnp.bfloat16)
    flat_images = weighted.reshape(num_rows, 2 * freqs)
    ctf_power = table * table * inverse
    translations = trans_ids[0]
    cosine, sine = phases(translations, freqs)
    full_sections = lax.all_gather(projections[0], "img", axis=3, tiled=True)
    piece = lax.all_gather(full_sections, "cls", axis=0, tiled=True)
    number = piece.shape[0]
    shifted = shift_sections(piece, inverse, cosine, sine).reshape(number * O * TR, 2 * freqs)
    cross_terms = contract_last(flat_images, shifted)
    norm_rows = jnp.dot(
        onehot,
        contract_high(ctf_power, section_power(piece)),
        precision=lax.Precision.HIGHEST,
        preferred_element_type=jnp.float32,
    )
    block = (
        cross_terms.reshape(num_rows, number, O, TR)
        - 0.5 * norm_rows.reshape(num_rows, number, O)[:, :, :, None]
    )
    allowed = jnp.any(
        orient_ids[0][:, :, None] == jnp.arange(O, dtype=jnp.int32)[None, None, :], axis=1
    )
    mask = jnp.broadcast_to(allowed[:, None, :, None], block.shape)
    top = jnp.max(jnp.where(mask, block, -jnp.inf), axis=(1, 2, 3), keepdims=True)
    expo = jnp.exp(jnp.where(mask, block - top, -jnp.inf))
    total = jnp.sum(expo, axis=(1, 2, 3), keepdims=True)
    live = (jnp.arange(num_rows, dtype=jnp.int32) < counts[0, 0]).astype(jnp.float32)
    weights = (expo / total * live[:, None, None, None]).astype(jnp.bfloat16)
    per_class = jnp.moveaxis(weights, 1, 0).reshape(K, num_rows, O * TR)

    def back_class(class_weights):
        summed = lax.dot_general(
            class_weights, flat_images, (((0,), (0,)), ((), ())), preferred_element_type=jnp.float32
        )
        summed = summed.reshape(O, TR, 2, freqs)
        slab_re = jnp.sum(summed[:, :, 0] * cosine + summed[:, :, 1] * sine, axis=1)
        slab_im = jnp.sum(summed[:, :, 1] * cosine - summed[:, :, 0] * sine, axis=1)
        return jnp.stack([slab_re, slab_im], axis=1)

    terms = lax.map(back_class, per_class)
    spread = lax.psum_scatter(terms, "img", scatter_dimension=3, tiled=True)
    own_slab = lax.psum_scatter(
        spread.astype(jnp.bfloat16), "cls", scatter_dimension=0, tiled=True
    ).astype(jnp.float32)
    partner = swapped(own_slab.astype(jnp.bfloat16), "half", 0).astype(own_slab.dtype)
    product = own_slab[:, :, 0] * partner[:, :, 0] + own_slab[:, :, 1] * partner[:, :, 1]
    return (weights.reshape(num_rows, K * O * TR)[None], own_slab[None], product[None])


def solution(mesh):
    return jax.shard_map(
        on_device,
        mesh=mesh,
        in_specs=(
            P("half", ("cls", "img"), None, None),
            P("half", "cls", None, None, "img"),
            P("half", None, None),
            P("half", ("cls", "img")),
            P("half", ("cls", "img"), None),
            P("half", None),
            P("half", None),
            P("half", ("cls", "img")),
        ),
        out_specs=(
            P("half", ("cls", "img"), None),
            P("half", "cls", None, None, "img"),
            P("half", "cls", None, "img"),
        ),
        check_vma=False,
    )
```

profile of v0, /device:TPU:1, one launch (start us, length us, event | category | flops | bytes accessed | tf_op | source)
XLA Modules:
  0.0 803.9 jit_solution(14484269285956258049)
XLA Ops:
  7.2 1.8 copy.37
  11.2 7.0 fusion.25
  18.2 9.1 %copy.56 = f32[256,8320]{0,1:T(8,128)} copy(f32[256,8320]{1,0:T(8,128)} %fusion.25) | data formatting | bytes 17039360
  27.3 24.2 %copy.41 = f32[1,256,2,8320]{1,3,2,0:T(8,128)} copy(bf16[1,256,2,8320]{3,2,1,0:T(2,128)(2,1)} %param.10) | data formatting | bytes 25559040 | tf_op jit(solution)/shard_map/convert_element_type | solution.py:79
  51.6 25.4 %fusion.14 = bf16[256,16640]{0,1:T(8,128)(2,1)} fusion(f32[1,256,2,8320]{1,3,2,0:T(8,128)} %copy.41, f32[256,8320]{0,1:T(8,128)} %copy.56), kind=kLoop, calls=%fused_computation.20 | loop fusion | flops 8519680 | bytes 34078720 | tf_op jit(solution)/shard_map/convert_element_type | solution.py:79
  78.2 11.5 %fusion.16 = bf16[256,2,8320,1,1]{2,1,0,4,3:T(2,128)(2,1)} fusion(f32[256,8320]{1,0:T(8,128)} %fusion.25, bf16[1,256,2,8320]{3,2,1,0:T(2,128)(2,1)} %param.10), kind=kLoop, calls=%fused_computation.25 | loop fusion | flops 12779520 | bytes 25559040 | tf_op jit(solution)/shard_map/convert_element_type | solution.py:79
  89.8 125.0 %all-gather.5.cloned.1.call-done = bf16[1,4,8,2,8320]{2,1,3,0,4:T(4,128)(2,1)} async-done(((bf16[1,4,8,2,130]{2,1,3,0,4:T(4,128)(2,1)}), bf16[1,4,8,2,8320]{2,1,3,0,4:T(4,128)(2,1)}) %all-gather.5.cloned.1.call-update) | async-done | bytes 1064976 | tf_op jit(solution)/shard_map/all_gather | solution.py:84
  214.8 19.8 %copy.38 = bf16[1,4,8,2,8320]{4,2,3,0,1:T(8,128)(2,1)} copy(bf16[1,4,8,2,8320]{2,1,3,0,4:T(4,128)(2,1)} %all-gather.5.cloned.1.call-done) | data formatting | bytes 2129920 | tf_op jit(solution)/shard_map/all_gather | solution.py:84
  235.7 34.9 %all-gather.7.cloned.1.call-done = bf16[1,8,8,2,8320]{4,2,3,0,1:T(8,128)(2,1)} async-done(((bf16[1,4,8,2,8320]{4,2,3,0,1:T(8,128)(2,1)}), bf16[1,8,8,2,8320]{4,2,3,0,1:T(8,128)(2,1)}) %all-gather.7.cloned.1.call-update) | async-done | bytes 2129936 | tf_op jit(solution)/shard_map/all_gather | solution.py:85
  270.6 2.0 fusion.18
  272.9 2.2 fusion.21
  275.4 7.4 subtract_convert_fusion
  282.8 10.9 %select_reduce_fusion = (f32[256]{0:T(256)S(1)}, f32[256,8,8,8,1]{0,3,4,2,1:T(8,128)S(1)}) fusion(f32[256,8,8]{0,2,1:T(8,128)S(1)} %bitcast.140, pred[256,8]{0,1:T(8,128)(4,1)S(1)} %fusion.54, bf16[8,8,8,1,8320]{4,2,3,1,0:T(8,128)(2,1)} %get-tuple-element.131, bf16[8,8,8,1,8320]{4,2,3,1,0:T(8,128)(2,1)} %get-tuple-element.130, ...), kind=kOutput, calls=%fused_computation.54 | convolution fusion | flops 4396548096 | bytes 26151936 | tf_op jit(solution)/shard_map/dot_general | solution.py:52
  294.0 83.4 %while.12 = (s32[]{:T(128)}, f32[8,8,2,8320]{3,1,2,0:T(8,128)}, bf16[8,256,64]{1,2,0:T(8,128)(2,1)S(1)}, bf16[256,16640]{0,1:T(8,128)(2,1)}, f32[8320]{0:T(1024)...) while((s32[]{:T(128)}, f32[8,8,2,8320]{3,1,2,0:T(8,128)}, ...), condition=%wide.region_6.7_spmd.clone.clone, body=%wide.region_3.6_spmd.clone.clone.sunk | while | flops 549785600 | bytes 21931680 | solution.py:119
  295.1 6.1 fusion.68
  301.2 1.5 add_reduce_fusion.2
  305.5 6.1 fusion.68
  311.6 1.5 add_reduce_fusion.2
  315.9 6.1 fusion.68
  322.0 1.5 add_reduce_fusion.2
  326.3 6.1 fusion.68
  332.4 1.5 add_reduce_fusion.2
  336.7 6.1 fusion.68
  342.9 1.5 add_reduce_fusion.2
  347.1 6.1 fusion.68
  353.3 1.5 add_reduce_fusion.2
  357.6 6.1 fusion.68
  363.7 1.5 add_reduce_fusion.2
  368.0 6.1 fusion.68
  374.1 1.5 add_reduce_fusion.2
  377.4 356.2 %all-reduce.2 = bf16[8,8,2,8320]{3,1,2,0:T(8,128)(2,1)S(1)} all-reduce(f32[8,8,2,8320]{3,1,2,0:T(8,128)} %get-tuple-element.35), channel_id=4, replica_groups=mesh['half'=2,'cls'=2,'img'=64] {'img'}, use_global_device_ids=true, to_apply=%region_7.8.clone | all-reduce | flops 1064960 | bytes 6389760
  735.3 58.8 %reduce-scatter.3.cloned.1.call-done = bf16[4,8,2,130]{3,1,2,0:T(8,128)(2,1)} async-done(((bf16[8,8,2,130]{3,1,2,0:T(8,128)(2,1)}), bf16[4,8,2,130]{3,1,2,0:T(8,128)(2,1)}) %reduce-scatter.3.cloned.1.call-update) | async-done | bytes 16656 | tf_op jit(solution)/shard_map/reduce_scatter | solution.py:121
  (76 shorter events, 30.9 us)
Async XLA Ops:
  7.2 207.6 %all-gather.5.cloned.1.call-start = ((), (), s32[]{:S(2)}) async-start(), calls=%async_computation.2 | async-start | bytes 17305600 | tf_op jit(solution)/shard_map/all_gather | solution.py:84
  9.1 261.5 %all-gather.7.cloned.1.call-start = ((), (), s32[]{:S(2)}) async-start(), calls=%async_computation.3 | async-start | bytes 3194880 | tf_op jit(solution)/shard_map/all_gather | solution.py:85
  27.3 24.2 %copy-start.2 = (f32[1,8320]{1,0:T(1,128)S(1)}, f32[1,8320]{1,0:T(1,128)}, u32[]{:S(2)}) copy-start(f32[1,8320]{1,0:T(1,128)} %param.16) | copy-start | bytes 99844
  51.6 25.4 %copy-start.4 = (u32[256]{0:T(256)S(1)}, u32[256]{0:T(256)}, u32[]{:S(2)}) copy-start(u32[256]{0:T(256)} %constant.79) | copy-start | bytes 3076
  234.6 38.1 %copy-start.1 = (f32[1,32,8320]{2,1,0:T(8,128)S(1)}, f32[1,32,8320]{2,1,0:T(8,128)}, u32[]{:S(2)}) copy-start(f32[1,32,8320]{2,1,0:T(8,128)} %param.12) | copy-start | bytes 3194884
  234.6 559.5 %reduce-scatter.3.cloned.1.call-start = ((), (), s32[]{:S(2)}) async-start(), calls=%async_computation.1 | async-start | bytes 98304 | tf_op jit(solution)/shard_map/reduce_scatter | solution.py:121
  270.6 2.2 copy-start
  270.6 4.5 copy-start.3
  794.1 2.6 collective-permute-start
Sparse Core Ops, SparseCore 0:
  11.4 203.2 all-gather.4
  234.7 35.8 all-gather.6
  734.4 59.6 reduce-scatter.2
where the time goes:
time: 806 us; the launch traced here: 804 us
  blocking collectives  356 us (44%)
  waiting for transfers between devices  219 us (27%)
  other arithmetic  75.1 us (9%)
  matrix products  69.3 us (9%)
  local copies, waits for them, and re-layouts  67.7 us (8%)
  between operations  15.2 us (2%)
    unnamed x1, blocking collectives  356 us
    all_gather x1, waiting for transfers between devices, on_device(): full_sections = lax.all_gather(projections[0], 'img', axis=3, tiled=True)  125 us
    reduce_scatter x1, waiting for transfers between devices, on_device(): lax.psum_scatter(spread.astype(jnp.bfloat16), 'cls', scatter_dimension=0,...  58.8 us
    dot_general x8, matrix products, back_class(): lax.dot_general(class_weights, flat_images, (((0,), (0,)), ((), ())), pre...  48.9 us
    convert_element_type x2, other arithmetic, on_device(): (ctf_rows[:, None, :] * images[0].astype(jnp.float32)).astype(jnp.bfloat16)  36.9 us
    all_gather x1, waiting for transfers between devices, on_device(): piece = lax.all_gather(full_sections, 'cls', axis=0, tiled=True)  34.9 us
    convert_element_type x1, local copies, waits for them, and re-layouts, on_device(): images[0].astype(jnp.float32)  24.2 us
    all_gather x1, local copies, waits for them, and re-layouts, on_device(): full_sections = lax.all_gather(projections[0], 'img', axis=3, tiled=True)  19.8 us
  transfers between devices with their start and end apart: 4, of which 3 were waited for; matrix products, arithmetic and copies ran while one was open for 10% of the time, Pallas kernels for 0%

commit v1 on v0

--- a/solution.py
+++ b/solution.py
@@ -81,7 +81,9 @@
     ctf_power = table * table * inverse
     translations = trans_ids[0]
     cosine, sine = phases(translations, freqs)
-    full_sections = lax.all_gather(projections[0], "img", axis=3, tiled=True)
+    full_sections = jnp.concatenate(
+        lax.all_to_all(jnp.stack([projections[0]] * lax.axis_size("img")), "img", 0, 0), axis=3
+    )
     piece = lax.all_gather(full_sections, "cls", axis=0, tiled=True)
     number = piece.shape[0]
     shifted = shift_sections(piece, inverse, cosine, sine).reshape(number * O * TR, 2 * freqs)

time: 806 us -> 685 us (0.85)
  waiting for transfers between devices: 219 us -> 97.8 us
  starting transfers between devices: 1.33 us -> 16.4 us
  local copies, waits for them, and re-layouts: 67.7 us -> 55.3 us
    all_gather x1 -> x0, waiting for transfers between devices: 125 us -> none  [on_device(): full_sections = lax.all_gather(projections[0], 'img', axis=3, tiled=True)]
    all_gather x1 -> x0, local copies, waits for them, and re-layouts: 19.8 us -> none  [on_device(): full_sections = lax.all_gather(projections[0], 'img', axis=3, tiled=True)]
    all_to_all x0 -> x1, starting transfers between devices: none -> 15.1 us  [on_device(): lax.all_to_all(jnp.stack([projections[0]] * lax.axis_size('img')), 'img',...]
  transfers between devices with their start and end apart: 4 -> 4, of which waited for: 3 -> 2; matrix products, arithmetic and copies ran while one was open for 10% -> 12% of each run, Pallas kernels for 0% -> 0%
where the time goes in v1:
time: 685 us; the launch traced here: 683 us
  blocking collectives  356 us (52%)
  waiting for transfers between devices  97.8 us (14%)
  other arithmetic  72.1 us (11%)
  matrix products  69.7 us (10%)
  local copies, waits for them, and re-layouts  55.3 us (8%)
  starting transfers between devices  16.4 us (2%)
  between operations  15.6 us (2%)
    unnamed x1, blocking collectives  356 us
    reduce_scatter x1, waiting for transfers between devices, on_device(): lax.psum_scatter(spread.astype(jnp.bfloat16), 'cls', scatter_dimension=0,...  58.8 us
    dot_general x8, matrix products, back_class(): lax.dot_general(class_weights, flat_images, (((0,), (0,)), ((), ())), pre...  48.9 us
    all_gather x1, waiting for transfers between devices, on_device(): piece = lax.all_gather(full_sections, 'cls', axis=0, tiled=True)  38.9 us
    convert_element_type x2, other arithmetic, on_device(): (ctf_rows[:, None, :] * images[0].astype(jnp.float32)).astype(jnp.bfloat16)  36.7 us
    convert_element_type x1, local copies, waits for them, and re-layouts, on_device(): images[0].astype(jnp.float32)  24.2 us
    all_to_all x1, starting transfers between devices, on_device(): lax.all_to_all(jnp.stack([projections[0]] * lax.axis_size('img')), 'img',...  15.1 us
  transfers between devices with their start and end apart: 4, of which 2 were waited for; matrix products, arithmetic and copies ran while one was open for 12% of the time, Pallas kernels for 0%

profile of v1, /device:TPU:1, one launch (start us, length us, event | category | flops | bytes accessed | tf_op | source)
XLA Modules:
  0.0 683.4 jit_solution(7758079763381279656)
XLA Ops:
  8.1 1.6 stack.18
  9.7 15.1 %all-to-all-start = ((bf16[64,4,8,2,130]{4,2,1,3,0:T(8,128)(2,1)}), bf16[64,4,8,2,130]{4,2,1,3,0:T(8,128)(2,1)S(1)}, u32[]{:S(2)}, u32[]{:S(2)}) async-start(bf16[64,4,8,2,130]{4,2,1,3,0:T(8,128)(2,1)} %stack.18), calls=%async_computation | async-start | bytes 4194304 | tf_op jit(solution)/shard_map/all_to_all | solution.py:85
  25.6 5.7 fusion.25
  31.4 9.1 %copy.77 = f32[256,8320]{0,1:T(8,128)} copy(f32[256,8320]{1,0:T(8,128)} %fusion.25) | data formatting | bytes 17039360
  40.5 24.2 %copy.62 = f32[1,256,2,8320]{1,3,2,0:T(8,128)} copy(bf16[1,256,2,8320]{3,2,1,0:T(2,128)(2,1)} %param.10) | data formatting | bytes 25559040 | tf_op jit(solution)/shard_map/convert_element_type | solution.py:79
  64.7 25.2 %fusion.14 = bf16[256,16640]{0,1:T(8,128)(2,1)} fusion(f32[1,256,2,8320]{1,3,2,0:T(8,128)} %copy.62, f32[256,8320]{0,1:T(8,128)} %copy.77), kind=kLoop, calls=%fused_computation.20 | loop fusion | flops 8519680 | bytes 34078720 | tf_op jit(solution)/shard_map/convert_element_type | solution.py:79
  91.2 11.5 %fusion.16 = bf16[256,2,8320,1,1]{2,1,0,4,3:T(2,128)(2,1)} fusion(f32[256,8320]{1,0:T(8,128)} %fusion.25, bf16[1,256,2,8320]{3,2,1,0:T(2,128)(2,1)} %param.10), kind=kLoop, calls=%fused_computation.25 | loop fusion | flops 12779520 | bytes 25559040 | tf_op jit(solution)/shard_map/convert_element_type | solution.py:79
  102.7 2.5 copy.59
  105.2 4.4 reshape.297
  110.8 38.9 %all-gather.2.cloned.1.call-done = bf16[8,8,2,8320]{3,1,2,0:T(8,128)(2,1)} async-done(((bf16[4,8,2,8320]{3,1,2,0:T(8,128)(2,1)}), bf16[8,8,2,8320]{3,1,2,0:T(8,128)(2,1)}) %all-gather.2.cloned.1.call-update) | async-done | bytes 2129936 | tf_op jit(solution)/shard_map/all_gather | solution.py:87
  149.7 3.9 fusion.21
  154.3 7.7 %subtract_convert_fusion = (bf16[8,8,8,1,8320]{4,2,3,1,0:T(8,128)(2,1)}, bf16[8,8,8,1,8320]{4,2,3,1,0:T(8,128)(2,1)}) fusion(f32[8,8320]{1,0:T(8,128)S(1)} %get-tuple-element.141, f32[8,8,8320]{2,1,0:T(8,128)S(1)} %get-tuple-element.139, f32[8,8320]{1,0:T(8,128)S(1)} %get-tuple-element.140, f32[8,8,8320]{2,1,0:T(8,128)S(1)} %get-tuple-element.138), kind=kLoop, calls=%fused_computation.24 | loop fusion | flops 34078720 | bytes 21831680 | tf_op jit(solution)/shard_map/convert.2
  161.9 10.9 %select_reduce_fusion = (f32[256]{0:T(256)S(1)}, f32[256,8,8,8,1]{0,3,4,2,1:T(8,128)S(1)}) fusion(f32[256,8,8]{0,2,1:T(8,128)S(1)} %bitcast.144, pred[256,8]{0,1:T(8,128)(4,1)S(1)} %fusion.54, bf16[8,8,8,1,8320]{4,2,3,1,0:T(8,128)(2,1)} %get-tuple-element.137, bf16[8,8,8,1,8320]{4,2,3,1,0:T(8,128)(2,1)} %get-tuple-element.136, ...), kind=kOutput, calls=%fused_computation.54 | convolution fusion | flops 4396548096 | bytes 26151936 | tf_op jit(solution)/shard_map/dot_general | solution.py:52
  173.1 83.4 %while.12 = (s32[]{:T(128)}, f32[8,8,2,8320]{3,1,2,0:T(8,128)}, bf16[8,256,64]{1,2,0:T(8,128)(2,1)S(1)}, bf16[256,16640]{0,1:T(8,128)(2,1)}, f32[8320]{0:T(1024)...) while((s32[]{:T(128)}, f32[8,8,2,8320]{3,1,2,0:T(8,128)}, ...), condition=%wide.region_6.7_spmd.clone.clone, body=%wide.region_3.6_spmd.clone.clone.sunk | while | flops 549785600 | bytes 21931680 | solution.py:121
  174.2 6.1 fusion.68
  180.3 1.5 add_reduce_fusion.2
  184.6 6.1 fusion.68
  190.7 1.5 add_reduce_fusion.2
  195.0 6.1 fusion.68
  201.1 1.5 add_reduce_fusion.2
  205.4 6.1 fusion.68
  211.6 1.5 add_reduce_fusion.2
  215.9 6.1 fusion.68
  222.0 1.5 add_reduce_fusion.2
  226.3 6.1 fusion.68
  232.4 1.5 add_reduce_fusion.2
  236.7 6.1 fusion.68
  242.8 1.5 add_reduce_fusion.2
  247.1 6.1 fusion.68
  253.2 1.5 add_reduce_fusion.2
  256.5 356.2 %all-reduce.2 = bf16[8,8,2,8320]{3,1,2,0:T(8,128)(2,1)S(1)} all-reduce(f32[8,8,2,8320]{3,1,2,0:T(8,128)} %get-tuple-element.35), channel_id=2, replica_groups=mesh['half'=2,'cls'=2,'img'=64] {'img'}, use_global_device_ids=true, to_apply=%region_7.8.clone | all-reduce | flops 1064960 | bytes 6389760
  614.4 58.8 %reduce-scatter.3.cloned.1.call-done = bf16[4,8,2,130]{3,1,2,0:T(8,128)(2,1)} async-done(((bf16[8,8,2,130]{3,1,2,0:T(8,128)(2,1)}), bf16[4,8,2,130]{3,1,2,0:T(8,128)(2,1)}) %reduce-scatter.3.cloned.1.call-update) | async-done | bytes 16656 | tf_op jit(solution)/shard_map/reduce_scatter | solution.py:123
  (81 shorter events, 30.4 us)
Async XLA Ops:
  7.2 17.7 %copy-start.5 = (s32[1,8]{1,0:T(1,128)S(1)}, s32[1,8]{1,0:T(1,128)}, u32[]{:S(2)}) copy-start(s32[1,8]{1,0:T(1,128)} %param.15) | copy-start | bytes 100
  7.2 17.8 %copy-start.4 = (s32[1,256,4]{1,2,0:T(4,128)S(1)}, s32[1,256,4]{1,2,0:T(4,128)}, u32[]{:S(2)}) copy-start(s32[1,256,4]{1,2,0:T(4,128)} %param.14) | copy-start | bytes 12292
  7.2 18.4 %copy-start.1 = (f32[1,32,8320]{2,1,0:T(8,128)S(1)}, f32[1,32,8320]{2,1,0:T(8,128)}, u32[]{:S(2)}) copy-start(f32[1,32,8320]{2,1,0:T(8,128)} %param.12) | copy-start | bytes 3194884
  7.2 18.4 %copy-start.3 = (s32[1,256]{1,0:T(1,128)S(1)}, s32[1,256]{1,0:T(1,128)}, u32[]{:S(2)}) copy-start(s32[1,256]{1,0:T(1,128)} %param.13) | copy-start | bytes 3076
  9.7 93.0 %all-to-all-start = ((bf16[64,4,8,2,130]{4,2,1,3,0:T(8,128)(2,1)}), bf16[64,4,8,2,130]{4,2,1,3,0:T(8,128)(2,1)S(1)}, u32[]{:S(2)}, u32[]{:S(2)}) async-start(bf16[64,4,8,2,130]{4,2,1,3,0:T(8,128)(2,1)} %stack.18), calls=%async_computation | async-start | bytes 4194304 | tf_op jit(solution)/shard_map/all_to_all | solution.py:85
  24.8 124.9 %all-gather.2.cloned.1.call-start = ((), (), s32[]{:S(2)}) async-start(), calls=%async_computation.2 | async-start | bytes 3194880 | tf_op jit(solution)/shard_map/all_gather | solution.py:87
  40.5 24.2 %copy-start.2 = (f32[1,8320]{1,0:T(1,128)S(1)}, f32[1,8320]{1,0:T(1,128)}, u32[]{:S(2)}) copy-start(f32[1,8320]{1,0:T(1,128)} %param.16) | copy-start | bytes 99844
  64.7 25.2 %copy-start.6 = (u32[256]{0:T(256)S(1)}, u32[256]{0:T(256)}, u32[]{:S(2)}) copy-start(u32[256]{0:T(256)} %constant.79) | copy-start | bytes 3076
  109.7 563.5 %reduce-scatter.3.cloned.1.call-start = ((), (), s32[]{:S(2)}) async-start(), calls=%async_computation.3 | async-start | bytes 98304 | tf_op jit(solution)/shard_map/reduce_scatter | solution.py:123
  149.7 4.3 copy-start
  673.2 2.6 collective-permute-start
Sparse Core Ops, SparseCore 0:
  109.8 39.8 all-gather.1
  613.6 59.6 reduce-scatter.2
